TPU v7x, 32 devices: a whole 2x2x4 slice. The times are simulated.
32 devices in a mesh: seg: 8 (over y, x, core), head: 4 (over z).
Axes of the slice: x: 2, y: 2, z: 4, core: 2. Of those that a mesh axis runs over, the one named last changes fastest.
Arguments:
- layer_input: bfloat16 [1, 4096, 2048], P(None, 'seg', 'head'), may hold values from -160 to 160, as said below
- w_qkv: bfloat16 [2048, 3, 1024], P(None, None, 'head'), may hold values from -3 to 3
- comp_weight: bfloat16 [3, 2, 1024], P(None, None, 'head'), may hold values from -2.5 to 2.5
- w_out: bfloat16 [1024, 2048], P('seg', 'head'), may hold values from -1.5 to 1.5
Outputs:
- attn_out: bfloat16 [1, 4096, 2048], P(None, 'seg', 'head')
Inputs may be any that keep to these rules, and one draw needn't show every extreme that they name: layer_input varies in scale from feature to feature and from token to token.
All inputs are finite; a program needn't handle non-finite values.
Results may differ from a plain program's by a relative error of at most 0.0089.
Values may be sent and summed in bfloat16 or wider, within the bound.
No kernel may reach another device: no remote copies, remote signals or barrier semaphores. Data moves between devices by JAX's collectives and lax.ppermute only.
A program may use at most 64 MiB of HBM per device.

v0:
```python
import math
import jax
import jax.numpy as jnp
from jax import lax
from jax.sharding import PartitionSpec as P

DH = 128


def passed_along(block, axis, distance):
    devices = range(lax.axis_size(axis))
    route = [(i - distance, i) for i in devices if i - distance in devices]
    return lax.ppermute(block, axis, route)


def layer_norm(values):
    center_mean = jnp.mean(values, axis=-1, keepdims=True)
    centered = values - center_mean
    variance = jnp.mean(centered * centered, axis=-1, keepdims=True)
    return centered * lax.rsqrt(variance + 1e-05)


def compress_block(source, weight):
    batch, pair, length, width = source.shape
    grouped = source.reshape(batch, pair, length // 3, 3, width)
    mixed = jnp.einsum("bkltc,tkc->bklc", grouped, weight, preferred_element_type=jnp.float32)
    return mixed.astype(jnp.bfloat16)


def key_allowed(seg_len, segment):
    query_pos = jnp.arange(seg_len)[:, None]
    key_pos = jnp.arange(3 * seg_len)[None, :]
    own_part = (key_pos >= 2 * seg_len) & (key_pos - 2 * seg_len <= query_pos)
    memory_part = (key_pos >= seg_len) & (key_pos < 2 * seg_len) & (segment >= 1)
    comp_part = (key_pos < seg_len) & (segment >= 4)
    return own_part | memory_part | comp_part


def attend(queries, key_vals, segment):
    batch, seg_len, width = queries.shape
    heads_here = width // DH
    query_heads = queries.reshape(batch, seg_len, heads_here, DH)
    key_heads = key_vals[:, 0].reshape(batch, 3 * seg_len, heads_here, DH)
    value_heads = key_vals[:, 1].reshape(batch, 3 * seg_len, heads_here, DH)
    scores = jnp.einsum(
        "bqhd,bkhd->bhqk", query_heads, key_heads, preferred_element_type=jnp.float32
    )
    scores = scores / math.sqrt(DH)
    allowed = key_allowed(seg_len, segment)
    scores = jnp.where(allowed[None, None], scores, jnp.float32(-1e30))
    highest = jnp.max(scores, axis=-1, keepdims=True)
    exponent = jnp.exp(scores - highest)
    weights = (exponent / jnp.sum(exponent, axis=-1, keepdims=True)).astype(jnp.bfloat16)
    mixed = jnp.einsum("bhqk,bkhd->bqhd", weights, value_heads, preferred_element_type=jnp.float32)
    return mixed.astype(jnp.bfloat16).reshape(batch, seg_len, width)


def local(layer_input, w_qkv, comp_weight, w_out):
    gathered = lax.all_gather(layer_input, "head", axis=2, tiled=True)
    normed = layer_norm(gathered.astype(jnp.float32)).astype(jnp.bfloat16)
    projected = jnp.einsum("bld,dkc->bklc", normed, w_qkv, preferred_element_type=jnp.float32)
    projected = projected.astype(jnp.bfloat16)
    queries = projected[:, 0]
    key_vals = projected[:, 1:3]
    memory = passed_along(key_vals, "seg", 1)
    second_back = passed_along(memory, "seg", 1)
    upcoming = compress_block(jnp.concatenate([second_back, memory, key_vals], axis=2), comp_weight)
    compressed = passed_along(upcoming, "seg", 2)
    segment = lax.axis_index("seg")
    joined = jnp.concatenate([compressed, memory, key_vals], axis=2)
    context = attend(queries, joined, segment)
    full_ctx = lax.all_gather(context, "head", axis=2, tiled=True)
    whole_out = lax.all_gather(w_out, "seg", axis=0, tiled=True)
    result_sum = jnp.einsum("blr,rc->blc", full_ctx, whole_out, preferred_element_type=jnp.float32)
    return result_sum.astype(jnp.bfloat16)


def solution(mesh):
    return jax.shard_map(
        local,
        mesh=mesh,
        in_specs=(
            P(None, "seg", "head"),
            P(None, None, "head"),
            P(None, None, "head"),
            P("seg", "head"),
        ),
        out_specs=P(None, "seg", "head"),
        check_vma=False,
    )
```

profile of v0, /device:TPU:0, one launch (start us, length us, event | category | flops | bytes accessed | tf_op | source)
XLA Modules:
  0.0 164.3 jit_solution(6512609901003673193)
XLA Ops:
  7.4 0.7 all-gather.4.cloned.1.call-update
  8.1 0.0 all-gather.8.cloned.1.call-start
  8.1 50.0 %all-gather.4.cloned.1.call-done = bf16[1,512,2048]{2,1,0:T(8,128)(2,1)} async-done(((bf16[1,512,512]{2,1,0:T(8,128)(2,1)}), bf16[1,512,2048]{2,1,0:T(8,128)(2,1)}) %all-gather.4.cloned.1.call-update) | async-done | bytes 2097168 | tf_op jit(solution)/shard_map/all_gather | solution.py:59
  58.2 2.1 %convert_reduce_fusion = f32[512]{0:T(512)S(1)} fusion(bf16[1,512,2048]{2,1,0:T(8,128)(2,1)} %all-gather.4.cloned.1.call-done), kind=kLoop, calls=%fused_computation.6 | loop fusion | flops 2096640 | bytes 2099200 | tf_op jit(solution)/shard_map/reduce_sum | solution.py:17
  60.3 0.1 copy-done.1
  60.4 0.7 fusion.4
  61.1 0.0 copy-start.4
  61.1 2.0 %fusion.21 = bf16[1,3,512,256]{2,3,1,0:T(8,128)(2,1)S(1)} fusion(bf16[2048,3,256]{2,0,1:T(8,128)(2,1)S(1)} %copy-done, bf16[1,512,2048]{2,1,0:T(8,128)(2,1)S(1)} %copy-done.1, f32[512]{0:T(512)S(1)} %add_rsqrt_fusion, f32[512]{0:T(512)S(1)} %broadcast_multiply_fusion), kind=kOutput, calls=%fused_computation.29 | convolution fusion | flops 1615200256 | bytes 6033408 | tf_op jit(solution)/shard_map/bld,dkc->bklc/dot_general | solution.py:61
  63.1 0.0 copy-start.2
  63.1 0.8 copy-done.2
  64.0 2.4 %collective-permute-start = (bf16[1,2,512,256]{2,3,1,0:T(8,128)(2,1)S(1)}, bf16[1,2,512,256]{2,3,1,0:T(8,128)(2,1)}, u32[]{:S(2)}, u32[]{:S(2)}) collective-permute-start(bf16[1,2,512,256]{2,3,1,0:T(8,128)(2,1)S(1)} %slice.16), channel_id=1, source_target_pairs={{0,4},{4,8},{8,12},{12,16},{16,20},{20,24},{24,28},{1,5},{5,9},{9,... | collective-permute-start | bytes 1572872 | tf_op jit(solution)/shard_map/ppermute | solution.py:13
  66.4 0.8 collective-permute-done
  67.2 9.1 %collective-permute-start.1 = (bf16[1,2,512,256]{2,3,1,0:T(8,128)(2,1)}, bf16[1,2,512,256]{2,3,1,0:T(8,128)(2,1)}, u32[]{:S(2)}, u32[]{:S(2)}) collective-permute-start(bf16[1,2,512,256]{2,3,1,0:T(8,128)(2,1)} %collective-permute-done), channel_id=1, source_target_pairs={{0,4},{4,8},{8,12},{12,16},{16,20},{20,24},{24,28},{1,5},{5,9},{9,... | collective-permute-start | bytes 1572872 | tf_op jit(solution)/shard_map/ppermute | solution.py:13
  76.3 0.0 all-gather.8.cloned.1.call-update
  76.3 0.0 all-gather.6.cloned.1.call-start
  76.4 0.9 collective-permute-done.1
  77.3 2.6 %pad_maximum_fusion.1 = bf16[1,2,1536,256]{2,3,1,0:T(8,128)(2,1)} fusion(bf16[1,2,512,256]{2,3,1,0:T(8,128)(2,1)} %copy-done.2, bf16[1,2,512,256]{2,3,1,0:T(8,128)(2,1)} %collective-permute-done, bf16[1,2,512,256]{2,3,1,0:T(8,128)(2,1)} %collective-permute-done.1), kind=kLoop, calls=%fused_computation.25 | loop fusion | flops 4718592 | bytes 3145728 | tf_op jit(solution)/shard_map/concatenate | solution.py:67
  80.0 4.9 %copy.23 = bf16[1,2,1536,256]{3,1,2,0:T(2,128)(2,1)} copy(bf16[1,2,1536,256]{2,3,1,0:T(8,128)(2,1)} %pad_maximum_fusion.1) | data formatting | bytes 3145728
  84.9 5.0 %multiply_reduce_fusion = bf16[2,256,512]{1,0,2:T(2,128)(2,1)} fusion(bf16[2,256,3,512]{1,0,2,3:T(2,128)(2,1)} %bitcast.45, f32[2,256,3]{1,0,2:T(2,128)S(1)} %bitcast_convert_fusion), kind=kLoop, calls=%fused_computation.11 | loop fusion | flops 2097152 | bytes 2103296
  89.9 2.0 %copy.20 = bf16[2,256,512]{2,1,0:T(8,128)(2,1)} copy(bf16[2,256,512]{1,0,2:T(2,128)(2,1)} %multiply_reduce_fusion) | data formatting | bytes 1048576 | tf_op jit(solution)/shard_map/bkltc,tkc->bklc/dot_general | solution.py:26
  91.9 11.8 %collective-permute-start.2 = (bf16[1,2,512,256]{2,3,1,0:T(8,128)(2,1)}, bf16[1,2,512,256]{2,3,1,0:T(8,128)(2,1)S(1)}, u32[]{:S(2)}, u32[]{:S(2)}) collective-permute-start(bf16[1,2,512,256]{2,3,1,0:T(8,128)(2,1)} %bitcast.49), channel_id=1, source_target_pairs={{0,8},{4,12},{8,16},{12,20},{16,24},{20,28},{1,9},{5,13},{9,17},{1... | collective-permute-start | bytes 1572872 | tf_op jit(solution)/shard_map/ppermute | solution.py:13
  103.7 1.6 fusion.10
  105.3 1.0 slice.18
  106.3 9.7 %collective-permute-done.2 = bf16[1,2,512,256]{2,3,1,0:T(8,128)(2,1)S(1)} collective-permute-done((bf16[1,2,512,256]{2,3,1,0:T(8,128)(2,1)}, bf16[1,2,512,256]{2,3,1,0:T(8,128)(2,1)S(1)}, u32[]{:S(2)}, u32[]{:S(2)}) %collective-permute-start.2) | collective-permute-done | bytes 524320 | tf_op jit(solution)/shard_map/ppermute | solution.py:13
  116.0 1.3 pad_maximum_fusion
  117.3 1.3 fusion.39
  118.6 3.8 %fusion.40 = f32[2,512]{1,0:T(2,128)S(1)} fusion(pred[512,1536]{1,0:T(8,128)(4,1)} %fusion.10, bf16[512,2,128]{0,2,1:T(8,128)(2,1)S(1)} %bitcast.50, bf16[1536,2,128]{0,2,1:T(8,128)(2,1)} %bitcast.46), kind=kOutput, calls=%fused_computation.53 | convolution fusion | flops 408946176 | bytes 1839104 | tf_op jit(solution)/shard_map/sub | solution.py:52
  122.5 5.2 %fusion.25 = bf16[2,128,512]{2,1,0:T(8,128)(2,1)} fusion(bf16[1536,2,128]{0,2,1:T(8,128)(2,1)} %bitcast.48, f32[2,512]{1,0:T(2,128)S(1)} %fusion.40, pred[512,1536]{1,0:T(8,128)(4,1)} %fusion.10, bf16[512,2,128]{0,2,1:T(8,128)(2,1)S(1)} %bitcast.51, bf16[1536,2,128]{0,2,1:T(8,128)(2,1)} %bitcast.47), kind=kOutput, calls=%fused_computation.32 | convolution fusion | flops 813304320 | bytes 2887680 | tf_op jit(solution)/shard_map/bhqk,bkhd->bqhd/dot_general | solution.py:54
  127.6 0.0 all-gather.6.cloned.1.call-update
  127.7 0.0 all-gather.8.cloned.1.call-done
  127.7 26.1 %all-gather.6.cloned.1.call-done = bf16[1,512,1024]{1,2,0:T(8,128)(2,1)} async-done(((bf16[1,512,256]{1,2,0:T(8,128)(2,1)}), bf16[1,512,1024]{1,2,0:T(8,128)(2,1)}) %all-gather.6.cloned.1.call-update) | async-done | bytes 1048592 | tf_op jit(solution)/shard_map/all_gather | solution.py:72
  153.8 3.1 %fusion.24 = bf16[1,512,512]{2,1,0:T(8,128)(2,1)} fusion(bf16[1024,512]{1,0:T(8,128)(2,1)} %all-gather.8.cloned.1.call-done, bf16[1,512,1024]{1,2,0:T(8,128)(2,1)} %all-gather.6.cloned.1.call-done), kind=kOutput, calls=%fused_computation.31 | convolution fusion | flops 537133056 | bytes 2621440 | tf_op jit(solution)/shard_map/blr,rc->blc/dot_general | solution.py:74
  (14 shorter events, 0.1 us)
Async XLA Ops:
  7.4 53.7 %copy-start = (bf16[2048,3,256]{2,0,1:T(8,128)(2,1)S(1)}, bf16[2048,3,256]{2,0,1:T(8,128)(2,1)}, u32[]{:S(2)}) copy-start(bf16[2048,3,256]{2,0,1:T(8,128)(2,1)} %param.5) | copy-start | bytes 9437188
  7.4 50.8 %all-gather.4.cloned.1.call-start = ((), (), s32[]{:S(2)}) async-start(), calls=%async_computation | async-start | bytes 2621440 | tf_op jit(solution)/shard_map/all_gather | solution.py:59
  8.1 119.6 %all-gather.8.cloned.1.call-start = ((), (), s32[]{:S(2)}) async-start(), calls=%async_computation.2 | async-start | bytes 1179648 | tf_op jit(solution)/shard_map/all_gather | solution.py:73
  58.1 2.2 %copy-start.1 = (bf16[1,512,2048]{2,1,0:T(8,128)(2,1)S(1)}, bf16[1,512,2048]{2,1,0:T(8,128)(2,1)}, u32[]{:S(2)}) copy-start(bf16[1,512,2048]{2,1,0:T(8,128)(2,1)} %all-gather.4.cloned.1.call-done) | copy-start | bytes 6291460
  61.1 15.3 %copy-start.4 = (bf16[3,2,256]{2,1,0:T(2,128)(2,1)S(1)}, bf16[3,2,256]{2,1,0:T(2,128)(2,1)}, u32[]{:S(2)}) copy-start(bf16[3,2,256]{2,1,0:T(2,128)(2,1)} %param.6) | copy-start | bytes 9220
  63.1 4.1 %copy-start.3 = (bf16[1,3,512,256]{2,3,1,0:T(8,128)(2,1)}, bf16[1,3,512,256]{2,3,1,0:T(8,128)(2,1)S(1)}, u32[]{:S(2)}) copy-start(bf16[1,3,512,256]{2,3,1,0:T(8,128)(2,1)S(1)} %fusion.21) | copy-start | bytes 2359300
  63.1 0.9 copy-start.2
  64.0 3.2 %collective-permute-start = (bf16[1,2,512,256]{2,3,1,0:T(8,128)(2,1)S(1)}, bf16[1,2,512,256]{2,3,1,0:T(8,128)(2,1)}, u32[]{:S(2)}, u32[]{:S(2)}) collective-permute-start(bf16[1,2,512,256]{2,3,1,0:T(8,128)(2,1)S(1)} %slice.16), channel_id=1, source_target_pairs={{0,4},{4,8},{8,12},{12,16},{16,20},{20,24},{24,28},{1,5},{5,9},{9,... | collective-permute-start | bytes 1572872 | tf_op jit(solution)/shard_map/ppermute | solution.py:13
  67.2 10.1 %collective-permute-start.1 = (bf16[1,2,512,256]{2,3,1,0:T(8,128)(2,1)}, bf16[1,2,512,256]{2,3,1,0:T(8,128)(2,1)}, u32[]{:S(2)}, u32[]{:S(2)}) collective-permute-start(bf16[1,2,512,256]{2,3,1,0:T(8,128)(2,1)} %collective-permute-done), channel_id=1, source_target_pairs={{0,4},{4,8},{8,12},{12,16},{16,20},{20,24},{24,28},{1,5},{5,9},{9,... | collective-permute-start | bytes 1572872 | tf_op jit(solution)/shard_map/ppermute | solution.py:13
  76.3 77.5 %all-gather.6.cloned.1.call-start = ((), (), s32[]{:S(2)}) async-start(), calls=%async_computation.1 | async-start | bytes 1310720 | tf_op jit(solution)/shard_map/all_gather | solution.py:72
  91.9 24.1 %collective-permute-start.2 = (bf16[1,2,512,256]{2,3,1,0:T(8,128)(2,1)}, bf16[1,2,512,256]{2,3,1,0:T(8,128)(2,1)S(1)}, u32[]{:S(2)}, u32[]{:S(2)}) collective-permute-start(bf16[1,2,512,256]{2,3,1,0:T(8,128)(2,1)} %bitcast.49), channel_id=1, source_target_pairs={{0,8},{4,12},{8,16},{12,20},{16,24},{20,28},{1,9},{5,13},{9,17},{1... | collective-permute-start | bytes 1572872 | tf_op jit(solution)/shard_map/ppermute | solution.py:13
Sparse Core Ops, SparseCore 0:
  9.7 48.3 all-gather.3
Sparse Core Ops, SparseCore 1:
  76.4 23.4 all-gather.7
  127.7 26.0 all-gather.5
where the time goes:
time: 165 us; the launch traced here: 164 us
  waiting for transfers between devices  88.4 us (54%)
  starting transfers between devices  23.3 us (14%)
  between operations  15 us (9%)
  matrix products  14.1 us (9%)
  other arithmetic  13.4 us (8%)
  local copies, waits for them, and re-layouts  10.2 us (6%)
    all_gather x1, waiting for transfers between devices, local(): gathered = lax.all_gather(layer_input, 'head', axis=2, tiled=True)  50 us
    all_gather x1, waiting for transfers between devices, local(): full_ctx = lax.all_gather(context, 'head', axis=2, tiled=True)  26.1 us
    ppermute x3, starting transfers between devices, passed_along(): return lax.ppermute(block, axis, route)  23.2 us
    ppermute x3, waiting for transfers between devices, passed_along(): return lax.ppermute(block, axis, route)  11.5 us
    unnamed x11, local copies, waits for them, and re-layouts  5.9 us
    dot_general x1, matrix products, attend(): jnp.einsum('bhqk,bkhd->bqhd', weights, value_heads, preferred_element_typ...  5.18 us
    unnamed x2, other arithmetic  5.02 us
    sub x1, matrix products, attend(): exponent = jnp.exp(scores - highest)  3.83 us
  transfers between devices with their start and end apart: 6, of which 5 were waited for; matrix products, arithmetic and copies ran while one was open for 18% of the time, Pallas kernels for 0%

commit v1 on v0

--- a/solution.py
+++ b/solution.py
@@ -69,7 +69,12 @@
     segment = lax.axis_index("seg")
     joined = jnp.concatenate([compressed, memory, key_vals], axis=2)
     context = attend(queries, joined, segment)
-    full_ctx = lax.all_gather(context, "head", axis=2, tiled=True)
+    ring = [context]
+    for hop in range(3):
+        ring.append(lax.ppermute(ring[-1], "head", [(dev, (dev + 1) % 4) for dev in range(4)]))
+    full_ctx = jnp.roll(
+        jnp.concatenate(ring[::-1], axis=2), (lax.axis_index("head") + 1) * ring[0].shape[2], axis=2
+    )
     whole_out = lax.all_gather(w_out, "seg", axis=0, tiled=True)
     result_sum = jnp.einsum("blr,rc->blc", full_ctx, whole_out, preferred_element_type=jnp.float32)
     return result_sum.astype(jnp.bfloat16)

time: 165 us -> 177 us (1.073)
  local copies, waits for them, and re-layouts: 10.2 us -> 21.4 us
  waiting for transfers between devices: 88.4 us -> 90.3 us
    ppermute x0 -> x3, waiting for transfers between devices: none -> 28 us  [local(): lax.ppermute(ring[-1], 'head', [(dev, (dev + 1) % 4) for dev in range(4)])]
    all_gather x1 -> x0, waiting for transfers between devices: 26.1 us -> none  [local(): full_ctx = lax.all_gather(context, 'head', axis=2, tiled=True)]
    unnamed x11 -> x24, local copies, waits for them, and re-layouts: 5.9 us -> 16.4 us
  transfers between devices with their start and end apart: 6 -> 8, of which waited for: 5 -> 7; matrix products, arithmetic and copies ran while one was open for 18% -> 22% of each run, Pallas kernels for 0% -> 0%
where the time goes in v1:
time: 177 us
  waiting for transfers between devices  90.3 us (51%)
  starting transfers between devices  23.3 us (13%)
  local copies, waits for them, and re-layouts  21.4 us (12%)
  between operations  15 us (8%)
  other arithmetic  13.4 us (8%)
  matrix products  13.4 us (8%)
    all_gather x1, waiting for transfers between devices, local(): gathered = lax.all_gather(layer_input, 'head', axis=2, tiled=True)  50 us
    ppermute x3, waiting for transfers between devices, local(): lax.ppermute(ring[-1], 'head', [(dev, (dev + 1) % 4) for dev in range(4)])  28 us
    ppermute x3, starting transfers between devices, passed_along(): return lax.ppermute(block, axis, route)  23.2 us
    unnamed x24, local copies, waits for them, and re-layouts  16.4 us
    ppermute x3, waiting for transfers between devices, passed_along(): return lax.ppermute(block, axis, route)  11.5 us
    unnamed x2, other arithmetic  5.04 us
    dot_general x1, matrix products, attend(): jnp.einsum('bhqk,bkhd->bqhd', weights, value_heads, preferred_element_typ...  4.55 us
    sub x1, matrix products, attend(): exponent = jnp.exp(scores - highest)  3.83 us
  transfers between devices with their start and end apart: 8, of which 7 were waited for; matrix products, arithmetic and copies ran while one was open for 22% of the time, Pallas kernels for 0%

profile of v1, /device:TPU:0, one launch (start us, length us, event | category | flops | bytes accessed | tf_op | source)
XLA Modules:
  0.0 176.8 jit_solution(14255322545353823871)
XLA Ops:
  8.1 50.0 %all-gather.3.cloned.1.call-done = bf16[1,512,2048]{2,1,0:T(8,128)(2,1)} async-done(((bf16[1,512,512]{2,1,0:T(8,128)(2,1)}), bf16[1,512,2048]{2,1,0:T(8,128)(2,1)}) %all-gather.3.cloned.1.call-update) | async-done | bytes 2097168 | tf_op jit(solution)/shard_map/all_gather | solution.py:59
  58.2 2.1 %convert_reduce_fusion = f32[512]{0:T(512)S(1)} fusion(bf16[1,512,2048]{2,1,0:T(8,128)(2,1)} %all-gather.3.cloned.1.call-done), kind=kLoop, calls=%fused_computation.6 | loop fusion | flops 2096640 | bytes 2099200 | tf_op jit(solution)/shard_map/reduce_sum | solution.py:17
  61.1 2.0 %fusion.21 = bf16[1,3,512,256]{2,3,1,0:T(8,128)(2,1)S(1)} fusion(bf16[2048,3,256]{2,0,1:T(8,128)(2,1)S(1)} %copy-done, bf16[1,512,2048]{2,1,0:T(8,128)(2,1)S(1)} %copy-done.1, f32[512]{0:T(512)S(1)} %add_rsqrt_fusion, f32[512]{0:T(512)S(1)} %broadcast_multiply_fusion), kind=kOutput, calls=%fused_computation.29 | convolution fusion | flops 1615200256 | bytes 6033408 | tf_op jit(solution)/shard_map/bld,dkc->bklc/dot_general | solution.py:61
  63.1 0.8 copy-done.2
  64.0 2.4 %collective-permute-start = (bf16[1,2,512,256]{2,3,1,0:T(8,128)(2,1)S(1)}, bf16[1,2,512,256]{2,3,1,0:T(8,128)(2,1)}, u32[]{:S(2)}, u32[]{:S(2)}) collective-permute-start(bf16[1,2,512,256]{2,3,1,0:T(8,128)(2,1)S(1)} %slice.16), channel_id=1, source_target_pairs={{0,4},{4,8},{8,12},{12,16},{16,20},{20,24},{24,28},{1,5},{5,9},{9,... | collective-permute-start | bytes 1572872 | tf_op jit(solution)/shard_map/ppermute | solution.py:13
  66.4 0.9 collective-permute-done
  67.2 9.1 %collective-permute-start.1 = (bf16[1,2,512,256]{2,3,1,0:T(8,128)(2,1)}, bf16[1,2,512,256]{2,3,1,0:T(8,128)(2,1)}, u32[]{:S(2)}, u32[]{:S(2)}) collective-permute-start(bf16[1,2,512,256]{2,3,1,0:T(8,128)(2,1)} %collective-permute-done), channel_id=1, source_target_pairs={{0,4},{4,8},{8,12},{12,16},{16,20},{20,24},{24,28},{1,5},{5,9},{9,... | collective-permute-start | bytes 1572872 | tf_op jit(solution)/shard_map/ppermute | solution.py:13
  76.4 1.0 collective-permute-done.1
  77.3 2.6 %pad_maximum_fusion.1 = bf16[1,2,1536,256]{2,3,1,0:T(8,128)(2,1)} fusion(bf16[1,2,512,256]{2,3,1,0:T(8,128)(2,1)} %copy-done.2, bf16[1,2,512,256]{2,3,1,0:T(8,128)(2,1)} %collective-permute-done, bf16[1,2,512,256]{2,3,1,0:T(8,128)(2,1)} %collective-permute-done.1), kind=kLoop, calls=%fused_computation.25 | loop fusion | flops 4718592 | bytes 3145728 | tf_op jit(solution)/shard_map/concatenate | solution.py:67
  80.0 4.9 %copy.23 = bf16[1,2,1536,256]{3,1,2,0:T(2,128)(2,1)} copy(bf16[1,2,1536,256]{2,3,1,0:T(8,128)(2,1)} %pad_maximum_fusion.1) | data formatting | bytes 3145728
  84.9 5.0 %multiply_reduce_fusion = bf16[2,256,512]{1,0,2:T(2,128)(2,1)} fusion(bf16[2,256,3,512]{1,0,2,3:T(2,128)(2,1)} %bitcast.45, f32[2,256,3]{1,0,2:T(2,128)S(1)} %bitcast_convert_fusion), kind=kLoop, calls=%fused_computation.11 | loop fusion | flops 2097152 | bytes 2103296
  89.9 2.0 %copy.20 = bf16[2,256,512]{2,1,0:T(8,128)(2,1)} copy(bf16[2,256,512]{1,0,2:T(2,128)(2,1)} %multiply_reduce_fusion) | data formatting | bytes 1048576 | tf_op jit(solution)/shard_map/bkltc,tkc->bklc/dot_general | solution.py:26
  91.9 11.8 %collective-permute-start.2 = (bf16[1,2,512,256]{2,3,1,0:T(8,128)(2,1)}, bf16[1,2,512,256]{2,3,1,0:T(8,128)(2,1)S(1)}, u32[]{:S(2)}, u32[]{:S(2)}) collective-permute-start(bf16[1,2,512,256]{2,3,1,0:T(8,128)(2,1)} %bitcast.52), channel_id=1, source_target_pairs={{0,8},{4,12},{8,16},{12,20},{16,24},{20,28},{1,9},{5,13},{9,17},{1... | collective-permute-start | bytes 1572872 | tf_op jit(solution)/shard_map/ppermute | solution.py:13
  103.7 1.6 fusion.10
  105.3 1.0 slice.18
  106.3 9.7 %collective-permute-done.2 = bf16[1,2,512,256]{2,3,1,0:T(8,128)(2,1)S(1)} collective-permute-done((bf16[1,2,512,256]{2,3,1,0:T(8,128)(2,1)}, bf16[1,2,512,256]{2,3,1,0:T(8,128)(2,1)S(1)}, u32[]{:S(2)}, u32[]{:S(2)}) %collective-permute-start.2) | collective-permute-done | bytes 524320 | tf_op jit(solution)/shard_map/ppermute | solution.py:13
  116.0 1.3 pad_maximum_fusion
  117.3 1.3 fusion.41
  118.6 3.8 %fusion.42 = f32[2,512]{1,0:T(2,128)S(1)} fusion(pred[512,1536]{1,0:T(8,128)(4,1)} %fusion.10, bf16[512,2,128]{0,2,1:T(8,128)(2,1)S(1)} %bitcast.53, bf16[1536,2,128]{0,2,1:T(8,128)(2,1)} %bitcast.49), kind=kOutput, calls=%fused_computation.63 | convolution fusion | flops 408946176 | bytes 1839104 | tf_op jit(solution)/shard_map/sub | solution.py:52
  122.4 4.6 %fusion.25 = bf16[2,128,512]{2,1,0:T(8,128)(2,1)S(1)} fusion(bf16[1536,2,128]{0,2,1:T(8,128)(2,1)} %bitcast.51, f32[2,512]{1,0:T(2,128)S(1)} %fusion.42, pred[512,1536]{1,0:T(8,128)(4,1)} %fusion.10, bf16[512,2,128]{0,2,1:T(8,128)(2,1)} %bitcast.54, bf16[1536,2,128]{0,2,1:T(8,128)(2,1)} %bitcast.50), kind=kOutput, calls=%fused_computation.32 | convolution fusion | flops 813304320 | bytes 2887680 | tf_op jit(solution)/shard_map/bhqk,bkhd->bqhd/dot_general | solution.py:54
  127.1 10.0 %collective-permute-done.3 = bf16[1,512,256]{1,2,0:T(8,128)(2,1)S(1)} collective-permute-done((bf16[1,512,256]{1,2,0:T(8,128)(2,1)S(1)}, bf16[1,512,256]{1,2,0:T(8,128)(2,1)S(1)}, u32[]{:S(2)}, u32[]{:S(2)}) %collective-permute-start.3) | collective-permute-done | bytes 262176 | tf_op jit(solution)/shard_map/ppermute | solution.py:74
  137.8 9.3 %collective-permute-done.4 = bf16[1,512,256]{1,2,0:T(8,128)(2,1)} collective-permute-done((bf16[1,512,256]{1,2,0:T(8,128)(2,1)S(1)}, bf16[1,512,256]{1,2,0:T(8,128)(2,1)}, u32[]{:S(2)}, u32[]{:S(2)}) %collective-permute-start.4) | collective-permute-done | bytes 262176 | tf_op jit(solution)/shard_map/ppermute | solution.py:74
  147.1 8.7 %collective-permute-done.5 = bf16[1,512,256]{1,2,0:T(8,128)(2,1)} collective-permute-done((bf16[1,512,256]{1,2,0:T(8,128)(2,1)}, bf16[1,512,256]{1,2,0:T(8,128)(2,1)}, u32[]{:S(2)}, u32[]{:S(2)}) %collective-permute-start.5) | collective-permute-done | bytes 262176 | tf_op jit(solution)/shard_map/ppermute | solution.py:74
  155.8 1.7 constant_dynamic-update-slice_fusion.7
  157.4 1.7 constant_dynamic-update-slice_fusion.6
  159.1 1.7 constant_dynamic-update-slice_fusion.5
  160.8 0.7 constant_dynamic-update-slice_fusion.4
  161.5 1.7 constant_dynamic-update-slice_fusion.3
  163.1 1.7 constant_dynamic-update-slice_fusion.2
  164.8 0.7 constant_dynamic-update-slice_fusion.1
  165.6 0.7 constant_dynamic-update-slice_fusion
  166.3 3.1 %fusion.24 = bf16[1,512,512]{2,1,0:T(8,128)(2,1)} fusion(bf16[1024,512]{1,0:T(8,128)(2,1)} %all-gather.5.cloned.1.call-done, bf16[1,512,2048]{1,2,0:T(8,128)(2,1)} %constant_dynamic-update-slice_fusion, s32[]{:T(128)S(6)} %select_n.20), kind=kOutput, calls=%fused_computation.31 | convolution fusion | flops 537133056 | bytes 2621444 | tf_op jit(solution)/shard_map/blr,rc->blc/dot_general | solution.py:79
  (31 shorter events, 2.4 us)
Async XLA Ops:
  7.4 53.7 %copy-start = (bf16[2048,3,256]{2,0,1:T(8,128)(2,1)S(1)}, bf16[2048,3,256]{2,0,1:T(8,128)(2,1)}, u32[]{:S(2)}) copy-start(bf16[2048,3,256]{2,0,1:T(8,128)(2,1)} %param.5) | copy-start | bytes 9437188
  7.4 50.8 %all-gather.3.cloned.1.call-start = ((), (), s32[]{:S(2)}) async-start(), calls=%async_computation | async-start | bytes 2621440 | tf_op jit(solution)/shard_map/all_gather | solution.py:59
  8.1 158.2 %all-gather.5.cloned.1.call-start = ((), (), s32[]{:S(2)}) async-start(), calls=%async_computation.1 | async-start | bytes 1179648 | tf_op jit(solution)/shard_map/all_gather | solution.py:78
  58.1 2.2 %copy-start.1 = (bf16[1,512,2048]{2,1,0:T(8,128)(2,1)S(1)}, bf16[1,512,2048]{2,1,0:T(8,128)(2,1)}, u32[]{:S(2)}) copy-start(bf16[1,512,2048]{2,1,0:T(8,128)(2,1)} %all-gather.3.cloned.1.call-done) | copy-start | bytes 6291460
  61.1 15.3 %copy-start.7 = (bf16[3,2,256]{2,1,0:T(2,128)(2,1)S(1)}, bf16[3,2,256]{2,1,0:T(2,128)(2,1)}, u32[]{:S(2)}) copy-start(bf16[3,2,256]{2,1,0:T(2,128)(2,1)} %param.6) | copy-start | bytes 9220
  63.1 4.1 %copy-start.5 = (bf16[1,3,512,256]{2,3,1,0:T(8,128)(2,1)}, bf16[1,3,512,256]{2,3,1,0:T(8,128)(2,1)S(1)}, u32[]{:S(2)}) copy-start(bf16[1,3,512,256]{2,3,1,0:T(8,128)(2,1)S(1)} %fusion.21) | copy-start | bytes 2359300
  63.1 0.9 copy-start.2
  64.0 3.2 %collective-permute-start = (bf16[1,2,512,256]{2,3,1,0:T(8,128)(2,1)S(1)}, bf16[1,2,512,256]{2,3,1,0:T(8,128)(2,1)}, u32[]{:S(2)}, u32[]{:S(2)}) collective-permute-start(bf16[1,2,512,256]{2,3,1,0:T(8,128)(2,1)S(1)} %slice.16), channel_id=1, source_target_pairs={{0,4},{4,8},{8,12},{12,16},{16,20},{20,24},{24,28},{1,5},{5,9},{9,... | collective-permute-start | bytes 1572872 | tf_op jit(solution)/shard_map/ppermute | solution.py:13
  67.2 10.1 %collective-permute-start.1 = (bf16[1,2,512,256]{2,3,1,0:T(8,128)(2,1)}, bf16[1,2,512,256]{2,3,1,0:T(8,128)(2,1)}, u32[]{:S(2)}, u32[]{:S(2)}) collective-permute-start(bf16[1,2,512,256]{2,3,1,0:T(8,128)(2,1)} %collective-permute-done), channel_id=1, source_target_pairs={{0,4},{4,8},{8,12},{12,16},{16,20},{20,24},{24,28},{1,5},{5,9},{9,... | collective-permute-start | bytes 1572872 | tf_op jit(solution)/shard_map/ppermute | solution.py:13
  91.9 24.1 %collective-permute-start.2 = (bf16[1,2,512,256]{2,3,1,0:T(8,128)(2,1)}, bf16[1,2,512,256]{2,3,1,0:T(8,128)(2,1)S(1)}, u32[]{:S(2)}, u32[]{:S(2)}) collective-permute-start(bf16[1,2,512,256]{2,3,1,0:T(8,128)(2,1)} %bitcast.52), channel_id=1, source_target_pairs={{0,8},{4,12},{8,16},{12,20},{16,24},{20,28},{1,9},{5,13},{9,17},{1... | collective-permute-start | bytes 1572872 | tf_op jit(solution)/shard_map/ppermute | solution.py:13
  106.3 12.3 %copy-start.6 = (bf16[1,1,512,256]{2,3,1,0:T(8,128)(2,1)}, bf16[1,1,512,256]{2,3,1,0:T(8,128)(2,1)S(1)}, u32[]{:S(2)}) copy-start(bf16[1,1,512,256]{2,3,1,0:T(8,128)(2,1)S(1)} %slice.18) | copy-start | bytes 786436
  127.0 10.1 %collective-permute-start.3 = (bf16[1,512,256]{1,2,0:T(8,128)(2,1)S(1)}, bf16[1,512,256]{1,2,0:T(8,128)(2,1)S(1)}, u32[]{:S(2)}, u32[]{:S(2)}) collective-permute-start(bf16[1,512,256]{1,2,0:T(8,128)(2,1)S(1)} %bitcast.46), channel_id=1, source_target_pairs={{0,1},{1,2},{2,3},{3,0},{4,5},{5,6},{6,7},{7,4},{8,9},{9,10},{10,1... | collective-permute-start | bytes 786440 | tf_op jit(solution)/shard_map/ppermute | solution.py:74
  137.1 0.7 copy-start.3
  137.8 9.3 %collective-permute-start.4 = (bf16[1,512,256]{1,2,0:T(8,128)(2,1)S(1)}, bf16[1,512,256]{1,2,0:T(8,128)(2,1)}, u32[]{:S(2)}, u32[]{:S(2)}) collective-permute-start(bf16[1,512,256]{1,2,0:T(8,128)(2,1)S(1)} %collective-permute-done.3), channel_id=1, source_target_pairs={{0,1},{1,2},{2,3},{3,0},{4,5},{5,6},{6,7},{7,4},{8,9},{9,10},{10,1... | collective-permute-start | bytes 786440 | tf_op jit(solution)/shard_map/ppermute | solution.py:74
  147.1 8.7 %collective-permute-start.5 = (bf16[1,512,256]{1,2,0:T(8,128)(2,1)}, bf16[1,512,256]{1,2,0:T(8,128)(2,1)}, u32[]{:S(2)}, u32[]{:S(2)}) collective-permute-start(bf16[1,512,256]{1,2,0:T(8,128)(2,1)} %collective-permute-done.4), channel_id=1, source_target_pairs={{0,1},{1,2},{2,3},{3,0},{4,5},{5,6},{6,7},{7,4},{8,9},{9,10},{10,1... | collective-permute-start | bytes 786440 | tf_op jit(solution)/shard_map/ppermute | solution.py:74
  147.1 17.7 %copy-start.4 = (bf16[1,512,256]{1,2,0:T(8,128)(2,1)S(1)}, bf16[1,512,256]{1,2,0:T(8,128)(2,1)}, u32[]{:S(2)}) copy-start(bf16[1,512,256]{1,2,0:T(8,128)(2,1)} %copy-done.3) | copy-start | bytes 786436
Sparse Core Ops, SparseCore 0:
  9.7 48.3 all-gather.2
Sparse Core Ops, SparseCore 1:
  76.4 23.4 all-gather.4
